TPU v7x, 256 devices: a whole 4x4x8 slice. The times are simulated.
256 devices in a mesh: shard: 64 (over x, z, core), rep: 4 (over y).
Axes of the slice: x: 4, y: 4, z: 8, core: 2. Of those that a mesh axis runs over, the one named last changes fastest.
Arguments:
- entities: bfloat16 [98304, 400], P(('shard', 'rep')), may hold values from -6 to 6
- row_state: float32 [98304], P(('shard', 'rep')), may hold values from 0.01 to 1
- relations: bfloat16 [512, 400], replicated, may hold values from -0.59765625 to 0.59765625
- requests: int32 [16384, 48], P(('shard', 'rep')), may hold values from -1 to 1535, as said below
- head_slots: int32 [768, 512], P(('shard', 'rep')), may hold values from 0 to 3071, as said below
- tail_slots: int32 [768, 512], P(('shard', 'rep')), may hold values from 0 to 3071, as said below
- neg_slots: int32 [768, 512], P(('shard', 'rep')), may hold values from 0 to 3071, as said below
- relation_ids: int32 [256, 3], P(('shard', 'rep')), may hold values from 0 to 511
Outputs:
- new_entities: bfloat16 [98304, 400], P(('shard', 'rep'))
- new_state: float32 [98304], P(('shard', 'rep'))
Inputs may be any that keep to these rules, and one draw needn't show every extreme that they name: `requests`: row r is device r // 64's list for peer r % 64 along shard: ids among that peer's 4 * 384 entity rows, or -1 for an empty entry. Live entries come first and are distinct within a list; every list has one live entry or more; every device fills some list, and in every draw some peer's lists are full from every device. `head_slots`: each value p * 48 + c names a live entry of the same device's list for peer p. `tail_slots`: each value p * 48 + c names a live entry of the same device's list for peer p. `neg_slots`: each value p * 48 + c names a live entry of the same device's list for peer p.
All inputs are finite; a program needn't handle non-finite values.
Results may differ from a plain program's by a relative error of at most 0.0035.
Values may be sent and summed in bfloat16 or wider, within the bound.
No kernel may reach another device: no remote copies, remote signals or barrier semaphores. Data moves between devices by JAX's collectives and lax.ppermute only.
A program may use at most 128 MiB of HBM per device.

v0:
```python
import jax
import jax.numpy as jnp
from jax import lax
from jax.sharding import PartitionSpec as P

learning_rate = 0.1


def span_free_grads(head_rows, tail_rows, neg_rows, relation):
    half_width = head_rows.shape[1] // 2
    head_real = head_rows[:, :half_width].astype(jnp.float32)
    head_imag = head_rows[:, half_width:].astype(jnp.float32)
    tail_real = tail_rows[:, :half_width].astype(jnp.float32)
    tail_imag = tail_rows[:, half_width:].astype(jnp.float32)
    rel_real = relation[:half_width].astype(jnp.float32)
    rel_imag = relation[half_width:].astype(jnp.float32)
    queries = jnp.concatenate(
        [head_real * rel_real - head_imag * rel_imag, head_real * rel_imag + head_imag * rel_real],
        axis=1,
    )
    probes = jnp.concatenate(
        [rel_real * tail_real + rel_imag * tail_imag, rel_real * tail_imag - rel_imag * tail_real],
        axis=1,
    )
    positives = jnp.sum(queries * tail_rows.astype(jnp.float32), axis=1)
    queries_low = queries.astype(jnp.bfloat16)
    probes_low = probes.astype(jnp.bfloat16)
    contract_last = (((1,), (1,)), ((), ()))
    contract_first = (((0,), (0,)), ((), ()))
    tail_scores = lax.dot_general(
        queries_low, neg_rows, contract_last, preferred_element_type=jnp.float32
    )
    head_scores = lax.dot_general(
        probes_low, neg_rows, contract_last, preferred_element_type=jnp.float32
    )
    neg_total = neg_rows.shape[0]
    positive_grad = -jax.nn.sigmoid(-positives)
    tail_weights = (jax.nn.sigmoid(tail_scores) / neg_total).astype(jnp.bfloat16)
    head_weights = (jax.nn.sigmoid(head_scores) / neg_total).astype(jnp.bfloat16)
    dquery = positive_grad[:, None] * tail_rows.astype(jnp.float32) + jnp.dot(
        tail_weights, neg_rows, preferred_element_type=jnp.float32
    )
    dprobe = jnp.dot(head_weights, neg_rows, preferred_element_type=jnp.float32)
    neg_grad = lax.dot_general(
        tail_weights, queries_low, contract_first, preferred_element_type=jnp.float32
    )
    neg_grad = neg_grad + lax.dot_general(
        head_weights, probes_low, contract_first, preferred_element_type=jnp.float32
    )
    dquery_real = dquery[:, :half_width]
    dquery_imag = dquery[:, half_width:]
    dprobe_real = dprobe[:, :half_width]
    dprobe_imag = dprobe[:, half_width:]
    head_grad = jnp.concatenate(
        [
            dquery_real * rel_real + dquery_imag * rel_imag,
            dquery_imag * rel_real - dquery_real * rel_imag,
        ],
        axis=1,
    )
    tail_grad = positive_grad[:, None] * queries + jnp.concatenate(
        [
            dprobe_real * rel_real - dprobe_imag * rel_imag,
            dprobe_real * rel_imag + dprobe_imag * rel_real,
        ],
        axis=1,
    )
    return (head_grad, tail_grad, neg_grad)


def local(
    entities, row_state, relations, requests, head_slots, tail_slots, neg_slots, relation_ids
):
    own_rows, row_width = entities.shape
    peer_count, slot_cap = requests.shape
    wanted = lax.all_to_all(requests, "shard", split_axis=0, concat_axis=0, tiled=True)
    live_mask = wanted >= 0
    slab_rows = lax.all_gather(entities, "rep", axis=0, tiled=True)
    served = jnp.where(
        live_mask[..., None], slab_rows[jnp.maximum(wanted, 0)], jnp.zeros((), entities.dtype)
    )
    fetched = lax.all_to_all(served, "shard", split_axis=0, concat_axis=0, tiled=True).reshape(
        peer_count * slot_cap, row_width
    )
    slot_grads = jnp.zeros((peer_count * slot_cap, row_width), jnp.float32)
    for block_index in range(head_slots.shape[0]):
        head_ids = head_slots[block_index]
        tail_ids = tail_slots[block_index]
        neg_ids = neg_slots[block_index]
        head_grad, tail_grad, neg_grad = span_free_grads(
            fetched[head_ids],
            fetched[tail_ids],
            fetched[neg_ids],
            relations[relation_ids[0, block_index]],
        )
        slot_grads = slot_grads.at[head_ids].add(head_grad)
        slot_grads = slot_grads.at[tail_ids].add(tail_grad)
        slot_grads = slot_grads.at[neg_ids].add(neg_grad)
    returned = lax.all_to_all(
        slot_grads.reshape(peer_count, slot_cap, row_width).astype(jnp.bfloat16),
        "shard",
        split_axis=0,
        concat_axis=0,
        tiled=True,
    ).astype(jnp.float32)
    slab_len = own_rows * lax.axis_size("rep")
    targets = jnp.where(live_mask, wanted, slab_len).reshape(-1)
    slab_grads = (
        jnp.zeros((slab_len, row_width), jnp.float32)
        .at[targets]
        .add(returned.reshape(-1, row_width), mode="drop")
    )
    row_grads = lax.psum_scatter(
        slab_grads.astype(jnp.bfloat16), "rep", scatter_dimension=0, tiled=True
    ).astype(jnp.float32)
    new_state = row_state + jnp.mean(row_grads * row_grads, axis=1)
    new_entities = (
        entities.astype(jnp.float32) - learning_rate * row_grads / jnp.sqrt(new_state)[:, None]
    ).astype(jnp.bfloat16)
    return (new_entities, new_state)


def solution(mesh):
    placed = (
        P(("shard", "rep"), None),
        P(("shard", "rep")),
        P(),
        P(("shard", "rep"), None),
        P(("shard", "rep"), None),
        P(("shard", "rep"), None),
        P(("shard", "rep"), None),
        P(("shard", "rep"), None),
    )
    return jax.shard_map(
        local,
        mesh=mesh,
        in_specs=placed,
        out_specs=(P(("shard", "rep"), None), P(("shard", "rep"))),
        check_vma=False,
    )
```

profile of v0, /device:TPU:2, one launch (start us, length us, event | category | flops | bytes accessed | tf_op | source)
XLA Modules:
  0.0 461.3 jit_solution(960907369169442283)
XLA Ops:
  7.2 1.9 copy.85
  9.9 20.4 %all_to_all.22 = s32[64,1,48]{2,1,0:T(1,128)S(1)} all-to-all(s32[64,1,48]{2,1,0:T(1,128)S(1)} %bitcast.77), channel_id=1, replica_groups=mesh['shard'=64,'rep'=4] {'shard'}, dimensions={0} | all-to-all | bytes 24576 | tf_op jit(solution)/shard_map/all_to_all | solution.py:76
  31.3 10.5 %all-gather.2.cloned.1.call-done = bf16[1536,400]{1,0:T(8,128)(2,1)} async-done(((bf16[384,400]{1,0:T(8,128)(2,1)}), bf16[1536,400]{1,0:T(8,128)(2,1)}) %all-gather.2.cloned.1.call-update) | async-done | bytes 1228816 | tf_op jit(solution)/shard_map/all_gather | solution.py:78
  41.8 12.8 %gather_fusion = bf16[3072,400]{1,0:T(8,128)(2,1)S(1)} fusion(bf16[1536,400]{1,0:T(8,128)(2,1)} %all-gather.2.cloned.1.call-done, s32[3072]{0:T(1024)S(1)} %broadcast_clamp_fusion), kind=kCustom, calls=%fused_computation | custom fusion | bytes 4927488 | tf_op jit(solution)/shard_map/gather | solution.py:80
  54.6 2.7 broadcast_select_fusion
  57.3 10.8 %all-to-all-start.1 = ((bf16[64,48,400]{2,1,0:T(8,128)(2,1)}), bf16[64,48,400]{2,1,0:T(8,128)(2,1)S(1)}, u32[]{:S(2)}, u32[]{:S(2)}) async-start(bf16[64,48,400]{2,1,0:T(8,128)(2,1)} %broadcast_select_fusion), calls=%async_computation.1 | async-start | bytes 6291456 | tf_op jit(solution)/shard_map/all_to_all | solution.py:82
  68.1 1.4 fusion.88
  82.6 57.4 %all-to-all-done.1 = bf16[64,48,400]{2,1,0:T(8,128)(2,1)S(1)} async-done(((bf16[64,48,400]{2,1,0:T(8,128)(2,1)}), bf16[64,48,400]{2,1,0:T(8,128)(2,1)S(1)}, u32[]{:S(2)}, u32[]{:S(2)}) %all-to-all-start.1) | async-done | bytes 2457632 | tf_op jit(solution)/shard_map/all_to_all | solution.py:82
  140.0 2.6 gather_fusion.3
  142.6 2.6 gather_fusion.2
  145.2 2.0 copy.94
  147.2 2.6 gather_fusion.1
  149.8 2.0 fusion.87
  151.8 1.8 copy.118
  154.4 2.6 gather_fusion.4
  157.0 2.0 fusion.86
  158.9 1.7 copy.120
  161.5 2.6 gather_fusion.5
  164.1 2.0 copy.102
  166.1 2.9 fusion.48
  169.0 1.4 fusion.35
  170.5 1.7 fusion.29
  173.7 1.3 fusion.63
  175.4 1.2 multiply_subtract_fusion.4
  177.6 2.5 copy.95
  180.1 2.5 maximum_add_fusion
  182.5 2.5 copy.98
  185.1 2.8 convolution_add_fusion.2
  187.9 2.5 copy.99
  190.4 2.9 gather_fusion.6
  193.4 1.3 fusion.36
  194.7 1.8 fusion.31
  197.8 1.3 fusion.66
  201.6 2.5 copy.103
  204.1 2.3 maximum_add_fusion.1
  206.5 2.5 copy.106
  208.9 2.8 convolution_add_fusion.1
  211.7 2.5 copy.107
  214.2 2.6 gather_fusion.9
  216.8 2.6 gather_fusion.8
  219.4 1.2 copy.110
  220.7 2.8 gather_fusion.7
  223.4 1.3 fusion.85
  226.2 1.7 fusion.33
  229.3 1.4 fusion.69
  231.7 1.3 copy.111
  233.4 1.7 convolution_add_fusion
  235.1 1.4 copy.115
  236.4 7.7 %scatter_custom_fusion = f32[3072,400]{1,0:T(8,128)} fusion(s32[512]{0:T(512)} %bitcast.96, f32[512,400]{1,0:T(8,128)} %copy.95, f32[]{:T(128)} %constant.10.clone.1), kind=kCustom, calls=%fused_computation.22 | custom fusion | flops 204800 | bytes 4915712 | tf_op jit(solution)/shard_map/scatter-add | solution.py:96
  244.1 9.2 %scatter_fusion = f32[3072,400]{1,0:T(8,128)} fusion(f32[3072,400]{1,0:T(8,128)} %scatter_custom_fusion, s32[512]{0:T(512)} %bitcast.93, f32[512,400]{1,0:T(8,128)S(1)} %copy-done.8), kind=kCustom, calls=%fused_computation.11 | custom fusion | flops 204800 | bytes 2459648 | tf_op jit(solution)/shard_map/scatter-add | solution.py:97
  253.3 9.1 %scatter_fusion.1 = f32[3072,400]{1,0:T(8,128)} fusion(f32[3072,400]{1,0:T(8,128)} %scatter_fusion, s32[512]{0:T(512)S(1)} %bitcast.89, f32[512,400]{1,0:T(8,128)S(1)} %copy-done.9), kind=kCustom, calls=%fused_computation.12 | custom fusion | flops 204800 | bytes 2459648 | tf_op jit(solution)/shard_map/scatter-add | solution.py:98
  262.4 9.1 %scatter_fusion.2 = f32[3072,400]{1,0:T(8,128)} fusion(f32[3072,400]{1,0:T(8,128)} %scatter_fusion.1, s32[512]{0:T(512)S(1)} %bitcast.91, f32[512,400]{1,0:T(8,128)S(1)} %copy-done.10), kind=kCustom, calls=%fused_computation.13 | custom fusion | flops 204800 | bytes 2459648 | tf_op jit(solution)/shard_map/scatter-add | solution.py:96
  271.5 9.2 %scatter_fusion.3 = f32[3072,400]{1,0:T(8,128)} fusion(f32[3072,400]{1,0:T(8,128)} %scatter_fusion.2, s32[512]{0:T(512)S(1)} %bitcast.87, f32[512,400]{1,0:T(8,128)S(1)} %copy-done.11), kind=kCustom, calls=%fused_computation.14 | custom fusion | flops 204800 | bytes 2459648 | tf_op jit(solution)/shard_map/scatter-add | solution.py:97
  280.7 9.1 %scatter_fusion.4 = f32[3072,400]{1,0:T(8,128)} fusion(f32[3072,400]{1,0:T(8,128)} %scatter_fusion.3, s32[512]{0:T(512)S(1)} %bitcast.83, f32[512,400]{1,0:T(8,128)S(1)} %copy-done.12), kind=kCustom, calls=%fused_computation.15 | custom fusion | flops 204800 | bytes 2459648 | tf_op jit(solution)/shard_map/scatter-add | solution.py:98
  289.8 9.0 %scatter_fusion.5 = f32[3072,400]{1,0:T(8,128)} fusion(f32[3072,400]{1,0:T(8,128)} %scatter_fusion.4, s32[512]{0:T(512)S(1)} %bitcast.85, f32[512,400]{1,0:T(8,128)S(1)} %copy-done.13), kind=kCustom, calls=%fused_computation.16 | custom fusion | flops 204800 | bytes 2459648 | tf_op jit(solution)/shard_map/scatter-add | solution.py:96
  298.8 9.1 %scatter_fusion.6 = f32[3072,400]{1,0:T(8,128)} fusion(f32[3072,400]{1,0:T(8,128)} %scatter_fusion.5, s32[512]{0:T(512)S(1)} %bitcast.81, f32[512,400]{1,0:T(8,128)S(1)} %copy.114), kind=kCustom, calls=%fused_computation.17 | custom fusion | flops 204800 | bytes 2459648 | tf_op jit(solution)/shard_map/scatter-add | solution.py:97
  307.9 9.2 %scatter_fusion.7 = f32[3072,400]{1,0:T(8,128)} fusion(f32[3072,400]{1,0:T(8,128)} %scatter_fusion.6, s32[512]{0:T(512)S(1)} %bitcast.79, f32[512,400]{1,0:T(8,128)S(1)} %copy-done.14), kind=kCustom, calls=%fused_computation.18 | custom fusion | flops 204800 | bytes 2459648 | tf_op jit(solution)/shard_map/scatter-add | solution.py:98
  317.1 4.9 %convert_element_type.134 = bf16[3072,400]{1,0:T(8,128)(2,1)} convert(f32[3072,400]{1,0:T(8,128)} %scatter_fusion.7) | non-fusion elementwise | flops 1228800 | bytes 7372800 | tf_op jit(solution)/shard_map/convert_element_type | solution.py:100
  322.0 7.2 %all-to-all-start.2 = ((bf16[64,48,400]{2,1,0:T(8,128)(2,1)}), bf16[64,48,400]{2,1,0:T(8,128)(2,1)S(1)}, u32[]{:S(2)}, u32[]{:S(2)}) async-start(bf16[64,48,400]{2,1,0:T(8,128)(2,1)} %bitcast.75), calls=%async_computation.2 | async-start | bytes 6291456 | tf_op jit(solution)/shard_map/all_to_all | solution.py:99
  330.6 70.5 %all-to-all-done.2 = bf16[64,48,400]{2,1,0:T(8,128)(2,1)S(1)} async-done(((bf16[64,48,400]{2,1,0:T(8,128)(2,1)}), bf16[64,48,400]{2,1,0:T(8,128)(2,1)S(1)}, u32[]{:S(2)}, u32[]{:S(2)}) %all-to-all-start.2) | async-done | bytes 2457632 | tf_op jit(solution)/shard_map/all_to_all | solution.py:99
  401.1 20.8 %scatter_custom_fusion.9 = f32[1536,400]{1,0:T(8,128)} fusion(s32[3072]{0:T(1024)S(1)} %bitcast.94, bf16[3072,400]{1,0:T(8,128)(2,1)S(1)} %bitcast.74, f32[]{:T(128)} %constant.10.clone.1), kind=kCustom, calls=%fused_computation.20 | custom fusion | flops 2457600 | bytes 5603332 | tf_op jit(solution)/shard_map/scatter-add | solution.py:111
  421.9 3.2 convert_element_type.136
  425.2 25.2 %reduce-scatter.2.cloned.1.call-done = bf16[384,400]{1,0:T(8,128)(2,1)} async-done(((bf16[1536,400]{1,0:T(8,128)(2,1)}), bf16[384,400]{1,0:T(8,128)(2,1)}) %reduce-scatter.2.cloned.1.call-update) | async-done | bytes 307216 | tf_op jit(solution)/shard_map/reduce_scatter | solution.py:113
  452.1 1.2 fusion.40
  (170 shorter events, 25.2 us)
Async XLA Ops:
  7.2 34.6 %all-gather.2.cloned.1.call-start = ((), (), s32[]{:S(2)}) async-start(), calls=%async_computation.4 | async-start | bytes 1966080 | tf_op jit(solution)/shard_map/all_gather | solution.py:78
  30.4 1.0 copy-start.27
  54.6 20.9 %copy-start.29 = (bf16[512,400]{0,1:T(8,128)(2,1)S(1)}, bf16[512,400]{0,1:T(8,128)(2,1)}, u32[]{:S(2)}) copy-start(bf16[512,400]{0,1:T(8,128)(2,1)} %param.10) | copy-start | bytes 1228804
  57.3 82.7 %all-to-all-start.1 = ((bf16[64,48,400]{2,1,0:T(8,128)(2,1)}), bf16[64,48,400]{2,1,0:T(8,128)(2,1)S(1)}, u32[]{:S(2)}, u32[]{:S(2)}) async-start(bf16[64,48,400]{2,1,0:T(8,128)(2,1)} %broadcast_select_fusion), calls=%async_computation.1 | async-start | bytes 6291456 | tf_op jit(solution)/shard_map/all_to_all | solution.py:82
  77.3 0.6 copy-start.40
  77.3 4.7 %copy-start.30 = (s32[512,1]{0,1:T(1,128)}, s32[512,1]{0,1:T(1,128)S(1)}, u32[]{:S(2)}) copy-start(s32[512,1]{0,1:T(1,128)S(1)} %get-tuple-element.49) | copy-start | bytes 6148
  77.3 4.7 %copy-start.34 = (s32[512,1]{0,1:T(1,128)}, s32[512,1]{0,1:T(1,128)S(1)}, u32[]{:S(2)}) copy-start(s32[512,1]{0,1:T(1,128)S(1)} %get-tuple-element.51) | copy-start | bytes 6148
  78.7 0.6 copy-start.44
  78.7 3.3 copy-start.32
  78.7 3.3 copy-start.38
  80.1 1.9 copy-start.36
  80.1 1.9 copy-start.42
  80.1 1.9 copy-start.55
  166.1 6.1 %copy-start.5 = (bf16[512,400]{1,0:T(8,128)(2,1)S(1)}, bf16[512,400]{1,0:T(8,128)(2,1)}, u32[]{:S(2)}) copy-start(bf16[512,400]{1,0:T(8,128)(2,1)} %gather_fusion.3) | copy-start | bytes 1228804
  169.0 3.8 copy-start.25
  169.0 3.9 copy-start.26
  169.0 4.3 copy-start.3
  169.0 4.3 copy-start.4
  172.2 2.8 copy-start.2
  172.2 3.2 copy-start.51
  172.2 3.2 copy-start.52
  172.9 0.8 copy-start.17
  173.7 1.3 copy-start.45
  193.3 3.3 copy-start.7
  193.4 3.3 copy-start.23
  193.4 3.3 copy-start.24
  194.7 3.0 copy-start
  196.6 2.5 copy-start.1
  196.6 2.9 copy-start.49
  196.6 2.9 copy-start.50
  197.3 1.8 copy-start.18
  197.7 1.3 copy-start.46
  206.4 7.8 %copy-start.53 = (s32[1024]{0:T(1024)S(1)}, s32[1024]{0:T(1024)}, u32[]{:S(2)}) copy-start(s32[1024]{0:T(1024)} %pad_clamp_fusion) | copy-start | bytes 12292
  206.4 10.4 %copy-start.54 = (s32[1024]{0:T(1024)S(1)}, s32[1024]{0:T(1024)}, u32[]{:S(2)}) copy-start(s32[1024]{0:T(1024)} %pad_clamp_fusion.1) | copy-start | bytes 12292
  223.4 4.4 copy-start.6
  226.0 2.6 copy-start.19
  226.0 2.6 copy-start.21
  227.9 3.3 copy-start.47
  227.9 3.3 copy-start.48
  228.5 0.8 copy-start.16
  231.1 2.2 copy-start.20
  231.2 2.2 copy-start.22
  233.0 11.1 %copy-start.8 = (f32[512,400]{1,0:T(8,128)S(1)}, f32[512,400]{1,0:T(8,128)}, u32[]{:S(2)}) copy-start(f32[512,400]{1,0:T(8,128)} %copy.98) | copy-start | bytes 2457604
  244.1 9.2 %copy-start.9 = (f32[512,400]{1,0:T(8,128)S(1)}, f32[512,400]{1,0:T(8,128)}, u32[]{:S(2)}) copy-start(f32[512,400]{1,0:T(8,128)} %copy.99) | copy-start | bytes 2457604
  244.1 9.2 %copy-start.41 = (s32[512,1]{0,1:T(1,128)S(1)}, s32[512,1]{0,1:T(1,128)}, u32[]{:S(2)}) copy-start(s32[512,1]{0,1:T(1,128)} %copy-done.40) | copy-start | bytes 6148
  253.3 9.1 %copy-start.10 = (f32[512,400]{1,0:T(8,128)S(1)}, f32[512,400]{1,0:T(8,128)}, u32[]{:S(2)}) copy-start(f32[512,400]{1,0:T(8,128)} %copy.103) | copy-start | bytes 2457604
  253.3 9.1 %copy-start.43 = (s32[512,1]{0,1:T(1,128)S(1)}, s32[512,1]{0,1:T(1,128)}, u32[]{:S(2)}) copy-start(s32[512,1]{0,1:T(1,128)} %copy-done.42) | copy-start | bytes 6148
  262.4 9.1 %copy-start.11 = (f32[512,400]{1,0:T(8,128)S(1)}, f32[512,400]{1,0:T(8,128)}, u32[]{:S(2)}) copy-start(f32[512,400]{1,0:T(8,128)} %copy.106) | copy-start | bytes 2457604
  262.4 9.1 %copy-start.39 = (s32[512,1]{0,1:T(1,128)S(1)}, s32[512,1]{0,1:T(1,128)}, u32[]{:S(2)}) copy-start(s32[512,1]{0,1:T(1,128)} %copy-done.38) | copy-start | bytes 6148
  271.5 9.3 %copy-start.12 = (f32[512,400]{1,0:T(8,128)S(1)}, f32[512,400]{1,0:T(8,128)}, u32[]{:S(2)}) copy-start(f32[512,400]{1,0:T(8,128)} %copy.107) | copy-start | bytes 2457604
  271.5 9.3 %copy-start.35 = (s32[512,1]{0,1:T(1,128)S(1)}, s32[512,1]{0,1:T(1,128)}, u32[]{:S(2)}) copy-start(s32[512,1]{0,1:T(1,128)} %copy-done.34) | copy-start | bytes 6148
  280.7 9.1 %copy-start.13 = (f32[512,400]{1,0:T(8,128)S(1)}, f32[512,400]{1,0:T(8,128)}, u32[]{:S(2)}) copy-start(f32[512,400]{1,0:T(8,128)} %copy.111) | copy-start | bytes 2457604
  280.7 9.1 %copy-start.37 = (s32[512,1]{0,1:T(1,128)S(1)}, s32[512,1]{0,1:T(1,128)}, u32[]{:S(2)}) copy-start(s32[512,1]{0,1:T(1,128)} %copy-done.36) | copy-start | bytes 6148
  289.8 9.0 %copy-start.33 = (s32[512,1]{0,1:T(1,128)S(1)}, s32[512,1]{0,1:T(1,128)}, u32[]{:S(2)}) copy-start(s32[512,1]{0,1:T(1,128)} %copy-done.32) | copy-start | bytes 6148
  298.8 9.1 %copy-start.14 = (f32[512,400]{1,0:T(8,128)S(1)}, f32[512,400]{1,0:T(8,128)}, u32[]{:S(2)}) copy-start(f32[512,400]{1,0:T(8,128)} %copy.115) | copy-start | bytes 2457604
  298.8 9.1 %copy-start.31 = (s32[512,1]{0,1:T(1,128)S(1)}, s32[512,1]{0,1:T(1,128)}, u32[]{:S(2)}) copy-start(s32[512,1]{0,1:T(1,128)} %copy-done.30) | copy-start | bytes 6148
  317.1 12.7 %copy-start.28 = (s32[64,1,48]{2,1,0:T(1,128)S(1)}, s32[64,1,48]{2,1,0:T(1,128)}, u32[]{:S(2)}) copy-start(s32[64,1,48]{2,1,0:T(1,128)} %copy-done.27) | copy-start | bytes 36868
  322.0 79.2 %all-to-all-start.2 = ((bf16[64,48,400]{2,1,0:T(8,128)(2,1)}), bf16[64,48,400]{2,1,0:T(8,128)(2,1)S(1)}, u32[]{:S(2)}, u32[]{:S(2)}) async-start(bf16[64,48,400]{2,1,0:T(8,128)(2,1)} %bitcast.75), calls=%async_computation.2 | async-start | bytes 6291456 | tf_op jit(solution)/shard_map/all_to_all | solution.py:99
  329.2 121.1 %reduce-scatter.2.cloned.1.call-start = ((), (), s32[]{:S(2)}) async-start(), calls=%async_computation.5 | async-start | bytes 1966080 | tf_op jit(solution)/shard_map/reduce_scatter | solution.py:113
  401.1 50.4 %copy-start.56 = (f32[384]{0:T(512)S(1)}, f32[384]{0:T(512)}, u32[]{:S(2)}) copy-start(f32[384]{0:T(512)} %param.9) | copy-start | bytes 4612
  401.1 50.9 %copy-start.15 = (bf16[384,400]{1,0:T(8,128)(2,1)S(1)}, bf16[384,400]{1,0:T(8,128)(2,1)}, u32[]{:S(2)}) copy-start(bf16[384,400]{1,0:T(8,128)(2,1)} %copy.85) | copy-start | bytes 921604
Sparse Core Ops, SparseCore 0:
  9.8 31.9 all-gather.1
  425.3 25.0 reduce-scatter.1
where the time goes:
time: 466 us; the launch traced here: 461 us
  waiting for transfers between devices  164 us (35%)
  other arithmetic  138 us (30%)
  local copies, waits for them, and re-layouts  79.2 us (17%)
  between operations  21 us (5%)
  matrix products  20.8 us (4%)
  blocking collectives  20.4 us (4%)
  starting transfers between devices  18.1 us (4%)
    all_to_all x1, waiting for transfers between devices, local(): lax.all_to_all(slot_grads.reshape(peer_count, slot_cap, row_width).astype...  70.5 us
    all_to_all x1, waiting for transfers between devices, local(): lax.all_to_all(served, 'shard', split_axis=0, concat_axis=0, tiled=True)  57.4 us
    scatter-add x3, other arithmetic, local(): slot_grads = slot_grads.at[tail_ids].add(tail_grad)  27.5 us
    scatter-add x3, other arithmetic, local(): slot_grads = slot_grads.at[neg_ids].add(neg_grad)  27.3 us
    scatter-add x3, other arithmetic, local(): slot_grads = slot_grads.at[head_ids].add(head_grad)  25.7 us
    reduce_scatter x1, waiting for transfers between devices, local(): lax.psum_scatter(slab_grads.astype(jnp.bfloat16), 'rep', scatter_dimensio...  25.2 us
    scatter-add x1, other arithmetic, local(): slab_grads = jnp.zeros((slab_len, row_width), jnp.float32).at[targets].ad...  20.8 us
    all_to_all x1, blocking collectives, local(): lax.all_to_all(requests, 'shard', split_axis=0, concat_axis=0, tiled=True)  20.4 us
  transfers between devices with their start and end apart: 4, of which 4 were waited for; matrix products, arithmetic and copies ran while one was open for 2% of the time, Pallas kernels for 0%

commit v1 on v0

v1 whole, which is shorter than its diff:
```python
import jax
import jax.numpy as jnp
from jax import lax
from jax.experimental import pallas as pl
from jax.experimental.pallas import tpu as pltpu
from jax.sharding import PartitionSpec as P

learning_rate = 0.1
LANES = 128
SPLIT = 256
WIDE = 2 * SPLIT
TILES = WIDE // LANES
VMEM_LIMIT = 60 * 1024 * 1024


def spread(rows):
    half = rows.shape[1] // 2
    pad = ((0, 0), (0, SPLIT - half))
    return jnp.concatenate([jnp.pad(rows[:, :half], pad), jnp.pad(rows[:, half:], pad)], axis=1)


def serve_kernel(wanted_ref, slab_ref, out_ref):
    peers, cap = wanted_ref.shape
    slab_len = slab_ref.shape[0]
    columns = wanted_ref[...].T
    iota = lax.broadcasted_iota(jnp.int32, (cap, slab_len), 1)
    picks = [
        jnp.where(columns[:, p : p + 1] == iota, 1.0, 0.0).astype(jnp.bfloat16) for p in range(peers)
    ]
    picked = jnp.concatenate(picks, axis=0)
    rows = jnp.dot(picked, slab_ref[...], preferred_element_type=jnp.float32)
    out_ref[...] = rows.astype(jnp.bfloat16).reshape(out_ref.shape)


def serve(wanted, slab):
    peers, cap = wanted.shape
    step = 8
    return pl.pallas_call(
        serve_kernel,
        grid=(peers // step,),
        in_specs=[
            pl.BlockSpec((step, cap), lambda i: (i, 0)),
            pl.BlockSpec(slab.shape, lambda i: (0, 0)),
        ],
        out_specs=pl.BlockSpec((step, cap, WIDE), lambda i: (i, 0, 0)),
        out_shape=jax.ShapeDtypeStruct((peers, cap, WIDE), jnp.bfloat16),
        compiler_params=pltpu.CompilerParams(vmem_limit_bytes=VMEM_LIMIT),
        name="serve",
    )(wanted, slab)


def collect_kernel(wanted_ref, rows_ref, out_ref):
    step = out_ref.shape[0]
    groups, lanes = wanted_ref.shape
    base = pl.program_id(0) * step
    iota = lax.broadcasted_iota(jnp.int32, (step, lanes), 0) + base
    picks = [
        jnp.where(wanted_ref[g : g + 1, :] == iota, 1.0, 0.0).astype(jnp.bfloat16) for g in range(groups)
    ]
    picked = jnp.concatenate(picks, axis=1)
    out_ref[...] = jnp.dot(picked, rows_ref[...], preferred_element_type=jnp.float32).astype(out_ref.dtype)


def collect(wanted, rows, slab_len):
    step = 256
    return pl.pallas_call(
        collect_kernel,
        grid=(slab_len // step,),
        in_specs=[
            pl.BlockSpec(wanted.shape, lambda i: (0, 0)),
            pl.BlockSpec(rows.shape, lambda i: (0, 0)),
        ],
        out_specs=pl.BlockSpec((step, WIDE), lambda i: (i, 0)),
        out_shape=jax.ShapeDtypeStruct((slab_len, WIDE), jnp.bfloat16),
        compiler_params=pltpu.CompilerParams(vmem_limit_bytes=VMEM_LIMIT),
        name="collect",
    )(wanted, rows)


def interleaved(ref, start, count):
    return [ref[pl.ds(start * TILES + k, count, stride=TILES), :] for k in range(TILES)]


def put_interleaved(ref, start, count, tiles):
    for k in range(TILES):
        ref[pl.ds(start * TILES + k, count, stride=TILES), :] = tiles[k]


def pair(tiles):
    return jnp.concatenate(tiles[:2], axis=1), jnp.concatenate(tiles[2:], axis=1)


def unpair(real, imag):
    return [real[:, :LANES], real[:, LANES:], imag[:, :LANES], imag[:, LANES:]]


def edge_kernel(
    head_ids, tail_ids, neg_ids, rel_ref, fetched_ref, out_ref,
    source, heads, tails, negs, sum_a, sum_b, sum_c, negs_low, pairs_low, weights_low,
):
    slots = fetched_ref.shape[0]
    blocks, edges = head_ids.shape
    chunk = 256

    @pl.loop(0, slots // chunk)
    def _(c):
        start = c * chunk
        block = fetched_ref[pl.ds(pl.multiple_of(start, chunk), chunk), :].astype(jnp.float32)
        put_interleaved(source, start, chunk, [block[:, k * LANES : (k + 1) * LANES] for k in range(TILES)])
        zeros = jnp.zeros((chunk * TILES, LANES), jnp.float32)
        for total in (sum_a, sum_b, sum_c):
            total[pl.ds(pl.multiple_of(start * TILES, chunk * TILES), chunk * TILES), :] = zeros

    @pl.loop(0, blocks)
    def _(b):
        unroll = 16

        @pl.loop(0, edges // unroll)
        def _(step):
            for u in range(unroll):
                j = step * unroll + u
                for ids, rows in ((head_ids, heads), (tail_ids, tails), (neg_ids, negs)):
                    at = pl.multiple_of(ids[b, j] * TILES, TILES)
                    rows[pl.ds(pl.multiple_of(j * TILES, TILES), TILES), :] = source[pl.ds(at, TILES), :]

        negs_low[...] = jnp.concatenate(
            [tile.astype(jnp.bfloat16) for tile in interleaved(negs, 0, edges)], axis=1
        )
        rel_re = rel_ref[pl.ds(b, 1), :SPLIT]
        rel_im = rel_ref[pl.ds(b, 1), SPLIT:]
        for c in range(edges // chunk):
            start = c * chunk
            head_re, head_im = pair(interleaved(heads, start, chunk))
            tail_re, tail_im = pair(interleaved(tails, start, chunk))
            query_re = head_re * rel_re - head_im * rel_im
            query_im = head_re * rel_im + head_im * rel_re
            probe_re = rel_re * tail_re + rel_im * tail_im
            probe_im = rel_re * tail_im - rel_im * tail_re
            positives = jnp.sum(query_re * tail_re + query_im * tail_im, axis=1, keepdims=True)
            positive_grad = -jax.nn.sigmoid(-positives)
            queries_low = jnp.concatenate([query_re, query_im], axis=1).astype(jnp.bfloat16)
            probes_low = jnp.concatenate([probe_re, probe_im], axis=1).astype(jnp.bfloat16)
            both = jnp.concatenate([queries_low, probes_low], axis=0)
            pairs_low[2 * start : 2 * start + 2 * chunk, :] = both
            scores = lax.dot_general(
                both, negs_low[...], (((1,), (1,)), ((), ())), preferred_element_type=jnp.float32
            )
            scale = 0.5 / edges
            weights = (jnp.tanh(scores * 0.5) * scale + scale).astype(jnp.bfloat16)
            weights_low[2 * start : 2 * start + 2 * chunk, :] = weights
            grads = jnp.dot(weights, negs_low[...], preferred_element_type=jnp.float32)
            dquery_re = positive_grad * tail_re + grads[:chunk, :SPLIT]
            dquery_im = positive_grad * tail_im + grads[:chunk, SPLIT:]
            dprobe_re = grads[chunk:, :SPLIT]
            dprobe_im = grads[chunk:, SPLIT:]
            put_interleaved(
                heads, start, chunk,
                unpair(dquery_re * rel_re + dquery_im * rel_im, dquery_im * rel_re - dquery_re * rel_im),
            )
            put_interleaved(
                tails, start, chunk,
                unpair(
                    positive_grad * query_re + dprobe_re * rel_re - dprobe_im * rel_im,
                    positive_grad * query_im + dprobe_re * rel_im + dprobe_im * rel_re,
                ),
            )
        neg_grad = lax.dot_general(
            weights_low[...], pairs_low[...], (((0,), (0,)), ((), ())), preferred_element_type=jnp.float32
        )
        put_interleaved(negs, 0, edges, [neg_grad[:, k * LANES : (k + 1) * LANES] for k in range(TILES)])

        @pl.loop(0, edges // unroll)
        def _(step):
            for u in range(unroll):
                j = step * unroll + u
                for ids, rows, total in (
                    (head_ids, heads, sum_a), (tail_ids, tails, sum_b), (neg_ids, negs, sum_c)
                ):
                    at = pl.multiple_of(ids[b, j] * TILES, TILES)
                    total[pl.ds(at, TILES), :] += rows[pl.ds(pl.multiple_of(j * TILES, TILES), TILES), :]

    @pl.loop(0, slots // chunk)
    def _(c):
        start = c * chunk
        parts = [interleaved(total, start, chunk) for total in (sum_a, sum_b, sum_c)]
        out_ref[pl.ds(pl.multiple_of(start, chunk), chunk), :] = jnp.concatenate(
            [(x + y + z).astype(jnp.bfloat16) for x, y, z in zip(*parts)], axis=1
        )


def edge_grads(head_ids, tail_ids, neg_ids, rel, fetched):
    slots = fetched.shape[0]
    edges = head_ids.shape[1]
    smem = pl.BlockSpec(memory_space=pltpu.SMEM)
    vmem = pl.BlockSpec(memory_space=pltpu.VMEM)
    rows = pltpu.VMEM((edges * TILES, LANES), jnp.float32)
    total = pltpu.VMEM((slots * TILES, LANES), jnp.float32)
    return pl.pallas_call(
        edge_kernel,
        in_specs=[smem, smem, smem, vmem, vmem],
        out_specs=vmem,
        out_shape=jax.ShapeDtypeStruct((slots, WIDE), jnp.bfloat16),
        scratch_shapes=[
            total, rows, rows, rows, total, total, total,
            pltpu.VMEM((edges, WIDE), jnp.bfloat16),
            pltpu.VMEM((2 * edges, WIDE), jnp.bfloat16),
            pltpu.VMEM((2 * edges, edges), jnp.bfloat16),
        ],
        compiler_params=pltpu.CompilerParams(vmem_limit_bytes=VMEM_LIMIT),
        name="edges",
    )(head_ids, tail_ids, neg_ids, rel, fetched)


def local(
    entities, row_state, relations, requests, head_slots, tail_slots, neg_slots, relation_ids
):
    own_rows, row_width = entities.shape
    half = row_width // 2
    peer_count, slot_cap = requests.shape
    slots = peer_count * slot_cap
    wanted = lax.all_to_all(requests, "shard", split_axis=0, concat_axis=0, tiled=True)
    slab = lax.all_gather(spread(entities), "rep", axis=0, tiled=True)
    served = serve(wanted, slab)
    fetched = lax.all_to_all(served, "shard", split_axis=0, concat_axis=0, tiled=True)
    rel = spread(relations[relation_ids[0]].astype(jnp.float32))
    slot_grads = edge_grads(head_slots, tail_slots, neg_slots, rel, fetched.reshape(slots, WIDE))
    returned = lax.all_to_all(
        slot_grads.reshape(peer_count, slot_cap, WIDE), "shard", split_axis=0, concat_axis=0, tiled=True
    )
    slab_len = slab.shape[0]
    slab_grads = collect(wanted.reshape(slots // LANES, LANES), returned.reshape(slots, WIDE), slab_len)
    row_grads = lax.psum_scatter(slab_grads, "rep", scatter_dimension=0, tiled=True).astype(jnp.float32)
    row_grads = jnp.concatenate([row_grads[:, :half], row_grads[:, SPLIT : SPLIT + half]], axis=1)
    new_state = row_state + jnp.mean(row_grads * row_grads, axis=1)
    new_entities = (
        entities.astype(jnp.float32) - learning_rate * row_grads / jnp.sqrt(new_state)[:, None]
    ).astype(jnp.bfloat16)
    return (new_entities, new_state)


def solution(mesh):
    placed = (
        P(("shard", "rep"), None),
        P(("shard", "rep")),
        P(),
        P(("shard", "rep"), None),
        P(("shard", "rep"), None),
        P(("shard", "rep"), None),
        P(("shard", "rep"), None),
        P(("shard", "rep"), None),
    )
    return jax.shard_map(
        local,
        mesh=mesh,
        in_specs=placed,
        out_specs=(P(("shard", "rep"), None), P(("shard", "rep"))),
        check_vma=False,
    )
```

time: 466 us -> 289 us (0.62)
  other arithmetic: 138 us -> 5.39 us
  local copies, waits for them, and re-layouts: 79.2 us -> 13.1 us
  Pallas kernels: 0 us -> 45.4 us
  matrix products: 20.8 us -> 0 us
  waiting for transfers between devices: 164 us -> 171 us
  between operations: 21 us -> 14.1 us
    scatter-add x10 -> x0, other arithmetic: 101 us -> none  [the longest x3 27.5 us: local(): slot_grads = slot_grads.at[tail_ids].add(tail_grad)]
    pallas_call x0 -> x3, Pallas kernels: none -> 45.4 us  [the longest x1 27.5 us: edge_grads(): pl.pallas_call(edge_kernel, in_specs=[smem, smem, smem, vmem, vmem], out_...]
    gather x13 -> x1, local copies, waits for them, and re-layouts: 42 us -> 1.67 us  [local(): rel = spread(relations[relation_ids[0]].astype(jnp.float32))]
    dot_general x18 -> x0, matrix products: 20.8 us -> none  [the longest x3 7.27 us: span_free_grads(): lax.dot_general(head_weights, probes_low, contract_first, preferred_eleme...]
    add x6 -> x0, local copies, waits for them, and re-layouts: 11.7 us -> none  [the longest x3 6.41 us: span_free_grads(): neg_grad + lax.dot_general(head_weights, probes_low, contract_first, pref...]
    all_to_all x1, waiting for transfers between devices: 57.4 us -> 67.5 us  [local(): lax.all_to_all(served, 'shard', split_axis=0, concat_axis=0, tiled=True)]
    convert_element_type x2 -> x1, other arithmetic: 8.15 us -> 0.01 us  [local(): rel = spread(relations[relation_ids[0]].astype(jnp.float32))]
    concatenate x3 -> x0, local copies, waits for them, and re-layouts: 6.24 us -> none  [span_free_grads(): jnp.concatenate([dquery_real * rel_real + dquery_imag * rel_imag, dquery_...]
  transfers between devices with their start and end apart: 4 -> 4, of which waited for: 4 -> 4; matrix products, arithmetic and copies ran while one was open for 2% -> 3% of each run, Pallas kernels for 0% -> 0%
where the time goes in v1:
time: 289 us; the launch traced here: 288 us
  waiting for transfers between devices  171 us (59%)
  Pallas kernels  45.4 us (16%)
  blocking collectives  20.4 us (7%)
  starting transfers between devices  18.1 us (6%)
  between operations  14.1 us (5%)
  local copies, waits for them, and re-layouts  13.1 us (5%)
  other arithmetic  5.39 us (2%)
    all_to_all x1, waiting for transfers between devices, local(): lax.all_to_all(slot_grads.reshape(peer_count, slot_cap, WIDE), 'shard', s...  67.8 us
    all_to_all x1, waiting for transfers between devices, local(): lax.all_to_all(served, 'shard', split_axis=0, concat_axis=0, tiled=True)  67.5 us
    pallas_call x1, Pallas kernels, edge_grads(): pl.pallas_call(edge_kernel, in_specs=[smem, smem, smem, vmem, vmem], out_...  27.5 us
    reduce_scatter x1, waiting for transfers between devices, local(): lax.psum_scatter(slab_grads, 'rep', scatter_dimension=0, tiled=True)  25.1 us
    all_to_all x1, blocking collectives, local(): lax.all_to_all(requests, 'shard', split_axis=0, concat_axis=0, tiled=True)  20.4 us
    all_gather x1, waiting for transfers between devices, local(): slab = lax.all_gather(spread(entities), 'rep', axis=0, tiled=True)  10.9 us
    all_to_all x1, starting transfers between devices, local(): lax.all_to_all(served, 'shard', split_axis=0, concat_axis=0, tiled=True)  10.7 us
    pallas_call x1, Pallas kernels, serve(): pl.pallas_call(serve_kernel, grid=(peers // step,), in_specs=[pl.BlockSpe...  9.32 us
  transfers between devices with their start and end apart: 4, of which 4 were waited for; matrix products, arithmetic and copies ran while one was open for 3% of the time, Pallas kernels for 0%

profile of v1, /device:TPU:2, one launch (start us, length us, event | category | flops | bytes accessed | tf_op | source)
XLA Modules:
  0.0 287.9 jit_solution(15341584698394744558)
XLA Ops:
  7.2 0.0 all-gather.2.cloned.1.call-start
  7.2 1.1 copy.22
  8.4 0.1 slice.31
  8.5 0.7 slice_select_fusion
  9.2 0.8 fusion.1
  9.9 0.0 all-gather.2.cloned.1.call-update
  10.0 0.8 copy.23
  10.8 20.4 %all_to_all.21 = s32[64,1,48]{2,1,0:T(1,128)} all-to-all(s32[64,1,48]{2,1,0:T(1,128)S(1)} %bitcast.13), channel_id=1, replica_groups=mesh['shard'=64,'rep'=4] {'shard'}, dimensions={0} | all-to-all | bytes 24576 | tf_op jit(solution)/shard_map/all_to_all | solution.py:221
  31.2 10.9 %all-gather.2.cloned.1.call-done.slab_ref = bf16[1536,512]{1,0:T(8,128)(2,1)} async-done(((bf16[384,512]{1,0:T(8,128)(2,1)}), bf16[1536,512]{1,0:T(8,128)(2,1)}) %all-gather.2.cloned.1.call-update) | async-done | bytes 1572880 | tf_op jit(solution)/shard_map/all_gather | solution.py:222
  42.1 9.3 %serve.1 = bf16[64,48,512]{2,1,0:T(8,128)(2,1)} custom-call(s32[64,48]{1,0:T(8,128)} %bitcast.12, bf16[1536,512]{1,0:T(8,128)(2,1)} %all-gather.2.cloned.1.call-done.slab_ref), custom_call_target="tpu_custom_call" | custom-call | tf_op jit(solution)/shard_map/serve/pallas_call | solution.py:38
  51.4 0.0 copy-start.4
  51.4 0.0 copy-start.2
  51.4 10.7 %all-to-all-start.1 = ((bf16[64,48,512]{2,1,0:T(8,128)(2,1)}), bf16[64,48,512]{2,1,0:T(8,128)(2,1)S(1)}, u32[]{:S(2)}, u32[]{:S(2)}) async-start(bf16[64,48,512]{2,1,0:T(8,128)(2,1)} %serve.1), calls=%async_computation.1 | async-start | bytes 6291456 | tf_op jit(solution)/shard_map/all_to_all | solution.py:224
  62.2 2.0 copy.24
  64.2 0.0 copy-done.4
  64.2 1.7 gather_fusion
  65.9 0.1 slice.29
  65.9 0.0 copy-done.2
  66.0 0.6 select_maximum_fusion.rel_ref
  66.6 67.5 %all-to-all-done.1 = bf16[64,48,512]{2,1,0:T(8,128)(2,1)S(1)} async-done(((bf16[64,48,512]{2,1,0:T(8,128)(2,1)}), bf16[64,48,512]{2,1,0:T(8,128)(2,1)S(1)}, u32[]{:S(2)}, u32[]{:S(2)}) %all-to-all-start.1) | async-done | bytes 3145760 | tf_op jit(solution)/shard_map/all_to_all | solution.py:224
  134.1 0.0 copy-start
  134.1 1.7 copy-done
  135.8 27.5 %edges.1 = bf16[3072,512]{1,0:T(8,128)(2,1)} custom-call(s32[3,512]{1,0:T(4,128)} %head_ids.1, s32[3,512]{1,0:T(4,128)} %tail_ids.1, s32[3,512]{1,0:T(4,128)} %neg_ids.1, f32[3,512]{1,0:T(4,128)} %select_maximum_fusion.rel_ref, bf16[3072,512]{1,0:T(8,128)(2,1)} %bitcast.9), custom_call_target="tpu_custom_call" | custom-call | tf_op jit(solution)/shard_map/edges/pallas_call | solution.py:198
  163.3 7.3 %all-to-all-start.2 = ((bf16[64,48,512]{2,1,0:T(8,128)(2,1)}), bf16[64,48,512]{2,1,0:T(8,128)(2,1)S(1)}, u32[]{:S(2)}, u32[]{:S(2)}) async-start(bf16[64,48,512]{2,1,0:T(8,128)(2,1)} %bitcast.10), calls=%async_computation.2 | async-start | bytes 6291456 | tf_op jit(solution)/shard_map/all_to_all | solution.py:227
  170.6 0.0 reduce-scatter.2.cloned.1.call-start
  170.7 0.5 broadcast.65
  171.2 2.1 reduce.3
  173.3 1.4 reshape.48.wanted_ref
  174.7 67.8 %all-to-all-done.2 = bf16[64,48,512]{2,1,0:T(8,128)(2,1)S(1)} async-done(((bf16[64,48,512]{2,1,0:T(8,128)(2,1)}), bf16[64,48,512]{2,1,0:T(8,128)(2,1)S(1)}, u32[]{:S(2)}, u32[]{:S(2)}) %all-to-all-start.2) | async-done | bytes 3145760 | tf_op jit(solution)/shard_map/all_to_all | solution.py:227
  242.6 0.0 copy-start.1
  242.6 1.6 copy-done.1
  244.2 8.5 %collect.1 = bf16[1536,512]{1,0:T(8,128)(2,1)} custom-call(s32[24,128]{1,0:T(8,128)} %reshape.48.wanted_ref, bf16[3072,512]{1,0:T(8,128)(2,1)} %bitcast.11), custom_call_target="tpu_custom_call" | custom-call | tf_op jit(solution)/shard_map/collect/pallas_call | solution.py:66
  252.7 0.0 copy-start.3
  252.7 0.0 reduce-scatter.2.cloned.1.call-update
  252.8 25.1 %reduce-scatter.2.cloned.1.call-done = bf16[384,512]{1,0:T(8,128)(2,1)} async-done(((bf16[1536,512]{1,0:T(8,128)(2,1)}), bf16[384,512]{1,0:T(8,128)(2,1)}) %reduce-scatter.2.cloned.1.call-update) | async-done | bytes 393232 | tf_op jit(solution)/shard_map/reduce_scatter | solution.py:232
  277.9 1.1 fusion.4
  279.0 0.3 multiply_reduce_fusion
  279.3 0.0 copy-done.3
  279.3 0.6 fusion.3
  279.9 0.3 subtract_convert_fusion
  280.2 0.9 copy.27
  (4 shorter events, 0.0 us)
Async XLA Ops:
  7.2 34.9 %all-gather.2.cloned.1.call-start = ((), (), s32[]{:S(2)}) async-start(), calls=%async_computation.4 | async-start | bytes 1966080 | tf_op jit(solution)/shard_map/all_gather | solution.py:222
  51.4 12.7 %copy-start.4 = (s32[1,3]{1,0:T(1,128)S(1)}, s32[1,3]{1,0:T(1,128)}, u32[]{:S(2)}) copy-start(s32[1,3]{1,0:T(1,128)} %param.15) | copy-start | bytes 40
  51.4 14.5 %copy-start.2 = (pred[256]{0:T(512)(128)(4,1)S(1)}, pred[256]{0:T(512)(128)(4,1)}, u32[]{:S(2)}) copy-start(pred[256]{0:T(512)(128)(4,1)} %constant.5.clone.1) | copy-start | bytes 772
  51.4 82.7 %all-to-all-start.1 = ((bf16[64,48,512]{2,1,0:T(8,128)(2,1)}), bf16[64,48,512]{2,1,0:T(8,128)(2,1)S(1)}, u32[]{:S(2)}, u32[]{:S(2)}) async-start(bf16[64,48,512]{2,1,0:T(8,128)(2,1)} %serve.1), calls=%async_computation.1 | async-start | bytes 6291456 | tf_op jit(solution)/shard_map/all_to_all | solution.py:224
  134.1 1.7 copy-start
  163.3 79.2 %all-to-all-start.2 = ((bf16[64,48,512]{2,1,0:T(8,128)(2,1)}), bf16[64,48,512]{2,1,0:T(8,128)(2,1)S(1)}, u32[]{:S(2)}, u32[]{:S(2)}) async-start(bf16[64,48,512]{2,1,0:T(8,128)(2,1)} %bitcast.10), calls=%async_computation.2 | async-start | bytes 6291456 | tf_op jit(solution)/shard_map/all_to_all | solution.py:227
  170.6 107.3 %reduce-scatter.2.cloned.1.call-start = ((), (), s32[]{:S(2)}) async-start(), calls=%async_computation.5 | async-start | bytes 1966080 | tf_op jit(solution)/shard_map/reduce_scatter | solution.py:232
  242.6 1.6 copy-start.1
  252.7 26.6 %copy-start.3 = (f32[384]{0:T(512)S(1)}, f32[384]{0:T(512)}, u32[]{:S(2)}) copy-start(f32[384]{0:T(512)} %param.9) | copy-start | bytes 4612
Sparse Core Ops, SparseCore 0:
  10.1 31.9 all-gather.1
  252.9 24.9 reduce-scatter.1

commit v2 on v1

--- a/solution.py
+++ b/solution.py
@@ -13,10 +13,30 @@
 VMEM_LIMIT = 60 * 1024 * 1024
 
 
+WIRE = 160
+GROUP = 16
+TAIL = 16
+
+
 def spread(rows):
     half = rows.shape[1] // 2
     pad = ((0, 0), (0, SPLIT - half))
     return jnp.concatenate([jnp.pad(rows[:, :half], pad), jnp.pad(rows[:, half:], pad)], axis=1)
+
+
+def wire_order(rows):
+    half = rows.shape[1] // 2
+    filler = jnp.zeros((rows.shape[0], WIDE - 2 * half), rows.dtype)
+    return jnp.concatenate(
+        [rows[:, :LANES], rows[:, half : half + LANES], rows[:, LANES:half], rows[:, half + LANES :], filler],
+        axis=1,
+    )
+
+
+def row_order(rows):
+    real = jnp.concatenate([rows[:, :LANES], rows[:, 256:328]], axis=1)
+    imag = jnp.concatenate([rows[:, LANES:256], rows[:, 328:400]], axis=1)
+    return jnp.concatenate([real, imag], axis=1)
 
 
 def serve_kernel(wanted_ref, slab_ref, out_ref):
@@ -29,7 +49,14 @@
     ]
     picked = jnp.concatenate(picks, axis=0)
     rows = jnp.dot(picked, slab_ref[...], preferred_element_type=jnp.float32)
-    out_ref[...] = rows.astype(jnp.bfloat16).reshape(out_ref.shape)
+    for k in range(3):
+        tile = rows[:, k * LANES : (k + 1) * LANES].astype(jnp.bfloat16).reshape(peers, cap, LANES)
+        out_ref[:, k * cap : (k + 1) * cap, :] = tile
+    tail = rows[:, 3 * LANES :].reshape(peers, cap // GROUP, GROUP, LANES)
+    packed = tail[:, 0]
+    for g in range(1, cap // GROUP):
+        packed = packed + pltpu.roll(tail[:, g], g * TAIL, axis=2)
+    out_ref[:, 3 * cap :, :] = packed.astype(jnp.bfloat16)
 
 
 def serve(wanted, slab):
@@ -42,36 +69,59 @@
             pl.BlockSpec((step, cap), lambda i: (i, 0)),
             pl.BlockSpec(slab.shape, lambda i: (0, 0)),
         ],
-        out_specs=pl.BlockSpec((step, cap, WIDE), lambda i: (i, 0, 0)),
-        out_shape=jax.ShapeDtypeStruct((peers, cap, WIDE), jnp.bfloat16),
+        out_specs=pl.BlockSpec((step, WIRE, LANES), lambda i: (i, 0, 0)),
+        out_shape=jax.ShapeDtypeStruct((peers, WIRE, LANES), jnp.bfloat16),
         compiler_params=pltpu.CompilerParams(vmem_limit_bytes=VMEM_LIMIT),
         name="serve",
     )(wanted, slab)
 
 
-def collect_kernel(wanted_ref, rows_ref, out_ref):
+def collect_kernel(wanted_ref, rows_ref, out_ref, rows_wide):
     step = out_ref.shape[0]
     groups, lanes = wanted_ref.shape
+    peers = rows_ref.shape[0]
+    cap = (WIRE - GROUP) // 3
     base = pl.program_id(0) * step
+
+    @pl.when(pl.program_id(0) == 0)
+    def _():
+        for k in range(3):
+            tile = rows_ref[:, k * cap : (k + 1) * cap, :]
+            rows_wide[:, k * LANES : (k + 1) * LANES] = tile.reshape(peers * cap, LANES)
+        packed = rows_ref[:, 3 * cap :, :].astype(jnp.float32)
+        lane = lax.broadcasted_iota(jnp.int32, packed.shape, 2)
+        tails = [
+            jnp.where((lane >= g * TAIL) & (lane < (g + 1) * TAIL), packed, 0.0).astype(jnp.bfloat16)
+            for g in range(cap // GROUP)
+        ]
+        rows_wide[:, 3 * LANES :] = jnp.concatenate(tails, axis=1).reshape(peers * cap, LANES)
+
     iota = lax.broadcasted_iota(jnp.int32, (step, lanes), 0) + base
     picks = [
         jnp.where(wanted_ref[g : g + 1, :] == iota, 1.0, 0.0).astype(jnp.bfloat16) for g in range(groups)
     ]
     picked = jnp.concatenate(picks, axis=1)
-    out_ref[...] = jnp.dot(picked, rows_ref[...], preferred_element_type=jnp.float32).astype(out_ref.dtype)
+    sums = jnp.dot(picked, rows_wide[...], preferred_element_type=jnp.float32)
+    tail = sums[:, 3 * LANES :]
+    tail = tail + pltpu.roll(tail, LANES - TAIL, axis=1) + pltpu.roll(tail, LANES - 2 * TAIL, axis=1)
+    lane = lax.broadcasted_iota(jnp.int32, tail.shape, 1)
+    tail = jnp.where(lane < TAIL, tail, 0.0)
+    out_ref[...] = jnp.concatenate([sums[:, : 3 * LANES], tail], axis=1).astype(out_ref.dtype)
 
 
 def collect(wanted, rows, slab_len):
     step = 256
+    slots = wanted.shape[0] * wanted.shape[1]
     return pl.pallas_call(
         collect_kernel,
         grid=(slab_len // step,),
         in_specs=[
             pl.BlockSpec(wanted.shape, lambda i: (0, 0)),
-            pl.BlockSpec(rows.shape, lambda i: (0, 0)),
+            pl.BlockSpec(rows.shape, lambda i: (0, 0, 0)),
         ],
         out_specs=pl.BlockSpec((step, WIDE), lambda i: (i, 0)),
         out_shape=jax.ShapeDtypeStruct((slab_len, WIDE), jnp.bfloat16),
+        scratch_shapes=[pltpu.VMEM((slots, WIDE), jnp.bfloat16)],
         compiler_params=pltpu.CompilerParams(vmem_limit_bytes=VMEM_LIMIT),
         name="collect",
     )(wanted, rows)
@@ -98,18 +148,33 @@
     head_ids, tail_ids, neg_ids, rel_ref, fetched_ref, out_ref,
     source, heads, tails, negs, sum_a, sum_b, sum_c, negs_low, pairs_low, weights_low,
 ):
-    slots = fetched_ref.shape[0]
+    peers = fetched_ref.shape[0]
+    cap = (WIRE - GROUP) // 3
+    groups = cap // GROUP
+    some = 8
+    span = some * cap
+    split = 72
+    early = LANES - split
     blocks, edges = head_ids.shape
     chunk = 256
 
-    @pl.loop(0, slots // chunk)
+    @pl.loop(0, peers // some)
     def _(c):
-        start = c * chunk
-        block = fetched_ref[pl.ds(pl.multiple_of(start, chunk), chunk), :].astype(jnp.float32)
-        put_interleaved(source, start, chunk, [block[:, k * LANES : (k + 1) * LANES] for k in range(TILES)])
-        zeros = jnp.zeros((chunk * TILES, LANES), jnp.float32)
+        at = pl.ds(c * some, some)
+        real, imag, tail = [
+            fetched_ref[at, k * cap : (k + 1) * cap, :].astype(jnp.float32).reshape(span, LANES) for k in range(3)
+        ]
+        packed = fetched_ref[at, 3 * cap :, :].astype(jnp.float32)
+        late = jnp.concatenate(
+            [pltpu.roll(packed, early - g * TAIL, axis=2) for g in range(groups)], axis=1
+        ).reshape(span, LANES)
+        lane = lax.broadcasted_iota(jnp.int32, (span, LANES), 1)
+        real_end = jnp.where(lane < split, tail, 0.0)
+        imag_end = jnp.where(lane < early, pltpu.roll(tail, early, axis=1), jnp.where(lane < split, late, 0.0))
+        put_interleaved(source, c * span, span, [real, real_end, imag, imag_end])
+        zeros = jnp.zeros((span * TILES, LANES), jnp.float32)
         for total in (sum_a, sum_b, sum_c):
-            total[pl.ds(pl.multiple_of(start * TILES, chunk * TILES), chunk * TILES), :] = zeros
+            total[pl.ds(pl.multiple_of(c * span * TILES, span * TILES), span * TILES), :] = zeros
 
     @pl.loop(0, blocks)
     def _(b):
@@ -179,17 +244,26 @@
                     at = pl.multiple_of(ids[b, j] * TILES, TILES)
                     total[pl.ds(at, TILES), :] += rows[pl.ds(pl.multiple_of(j * TILES, TILES), TILES), :]
 
-    @pl.loop(0, slots // chunk)
+    @pl.loop(0, peers // some)
     def _(c):
-        start = c * chunk
-        parts = [interleaved(total, start, chunk) for total in (sum_a, sum_b, sum_c)]
-        out_ref[pl.ds(pl.multiple_of(start, chunk), chunk), :] = jnp.concatenate(
-            [(x + y + z).astype(jnp.bfloat16) for x, y, z in zip(*parts)], axis=1
-        )
+        at = pl.ds(c * some, some)
+        parts = [interleaved(total, c * span, span) for total in (sum_a, sum_b, sum_c)]
+        real, real_end, imag, imag_end = [x + y + z for x, y, z in zip(*parts)]
+        lane = lax.broadcasted_iota(jnp.int32, (span, LANES), 1)
+        tail = jnp.where(lane < split, real_end, pltpu.roll(imag_end, split, axis=1))
+        for k, tile in enumerate((real, imag, tail)):
+            out_ref[at, k * cap : (k + 1) * cap, :] = tile.astype(jnp.bfloat16).reshape(some, cap, LANES)
+        late = imag_end.reshape(some, groups, GROUP, LANES)
+        lane = lax.broadcasted_iota(jnp.int32, (some, GROUP, LANES), 2)
+        packed = jnp.zeros((some, GROUP, LANES), jnp.float32)
+        for g in range(groups):
+            moved = pltpu.roll(late[:, g], split + g * TAIL, axis=2)
+            packed = jnp.where((lane >= g * TAIL) & (lane < (g + 1) * TAIL), moved, packed)
+        out_ref[at, 3 * cap :, :] = packed.astype(jnp.bfloat16)
 
 
 def edge_grads(head_ids, tail_ids, neg_ids, rel, fetched):
-    slots = fetched.shape[0]
+    slots = fetched.shape[0] * ((WIRE - GROUP) // 3)
     edges = head_ids.shape[1]
     smem = pl.BlockSpec(memory_space=pltpu.SMEM)
     vmem = pl.BlockSpec(memory_space=pltpu.VMEM)
@@ -199,7 +273,7 @@
         edge_kernel,
         in_specs=[smem, smem, smem, vmem, vmem],
         out_specs=vmem,
-        out_shape=jax.ShapeDtypeStruct((slots, WIDE), jnp.bfloat16),
+        out_shape=jax.ShapeDtypeStruct(fetched.shape, jnp.bfloat16),
         scratch_shapes=[
             total, rows, rows, rows, total, total, total,
             pltpu.VMEM((edges, WIDE), jnp.bfloat16),
@@ -214,23 +288,18 @@
 def local(
     entities, row_state, relations, requests, head_slots, tail_slots, neg_slots, relation_ids
 ):
-    own_rows, row_width = entities.shape
-    half = row_width // 2
     peer_count, slot_cap = requests.shape
     slots = peer_count * slot_cap
     wanted = lax.all_to_all(requests, "shard", split_axis=0, concat_axis=0, tiled=True)
-    slab = lax.all_gather(spread(entities), "rep", axis=0, tiled=True)
+    slab = lax.all_gather(wire_order(entities), "rep", axis=0, tiled=True)
     served = serve(wanted, slab)
     fetched = lax.all_to_all(served, "shard", split_axis=0, concat_axis=0, tiled=True)
     rel = spread(relations[relation_ids[0]].astype(jnp.float32))
-    slot_grads = edge_grads(head_slots, tail_slots, neg_slots, rel, fetched.reshape(slots, WIDE))
-    returned = lax.all_to_all(
-        slot_grads.reshape(peer_count, slot_cap, WIDE), "shard", split_axis=0, concat_axis=0, tiled=True
-    )
-    slab_len = slab.shape[0]
-    slab_grads = collect(wanted.reshape(slots // LANES, LANES), returned.reshape(slots, WIDE), slab_len)
-    row_grads = lax.psum_scatter(slab_grads, "rep", scatter_dimension=0, tiled=True).astype(jnp.float32)
-    row_grads = jnp.concatenate([row_grads[:, :half], row_grads[:, SPLIT : SPLIT + half]], axis=1)
+    slot_grads = edge_grads(head_slots, tail_slots, neg_slots, rel, fetched)
+    returned = lax.all_to_all(slot_grads, "shard", split_axis=0, concat_axis=0, tiled=True)
+    slab_grads = collect(wanted.reshape(slots // LANES, LANES), returned, slab.shape[0])
+    row_grads = lax.psum_scatter(slab_grads, "rep", scatter_dimension=0, tiled=True)
+    row_grads = row_order(row_grads).astype(jnp.float32)
     new_state = row_state + jnp.mean(row_grads * row_grads, axis=1)
     new_entities = (
         entities.astype(jnp.float32) - learning_rate * row_grads / jnp.sqrt(new_state)[:, None]

time: 289 us -> 269 us (0.931)
  waiting for transfers between devices: 171 us -> 154 us
    all_to_all x1, waiting for transfers between devices: 67.5 us -> 58.1 us  [local(): lax.all_to_all(served, 'shard', split_axis=0, concat_axis=0, tiled=True)]
    all_to_all x1, waiting for transfers between devices: 67.8 us -> 58.6 us  [local(): lax.all_to_all(slot_grads, 'shard', split_axis=0, concat_axis=0, tiled=True)]
    unnamed x14 -> x18, local copies, waits for them, and re-layouts: 8.2 us -> 6.36 us
  transfers between devices with their start and end apart: 4 -> 4, of which waited for: 4 -> 4; matrix products, arithmetic and copies ran while one was open for 3% -> 2% of each run, Pallas kernels for 0% -> 0%
where the time goes in v2:
time: 269 us
  waiting for transfers between devices  154 us (57%)
  Pallas kernels  48.1 us (18%)
  blocking collectives  20.5 us (8%)
  starting transfers between devices  18.2 us (7%)
  between operations  14.2 us (5%)
  local copies, waits for them, and re-layouts  11.4 us (4%)
    all_to_all x1, waiting for transfers between devices, local(): lax.all_to_all(slot_grads, 'shard', split_axis=0, concat_axis=0, tiled=True)  58.6 us
    all_to_all x1, waiting for transfers between devices, local(): lax.all_to_all(served, 'shard', split_axis=0, concat_axis=0, tiled=True)  58.1 us
    pallas_call x1, Pallas kernels, edge_grads(): pl.pallas_call(edge_kernel, in_specs=[smem, smem, smem, vmem, vmem], out_...  29 us
    reduce_scatter x1, waiting for transfers between devices, local(): lax.psum_scatter(slab_grads, 'rep', scatter_dimension=0, tiled=True)  25.2 us
    all_to_all x1, blocking collectives, local(): lax.all_to_all(requests, 'shard', split_axis=0, concat_axis=0, tiled=True)  20.5 us
    all_gather x1, waiting for transfers between devices, local(): slab = lax.all_gather(wire_order(entities), 'rep', axis=0, tiled=True)  11.6 us
    all_to_all x1, starting transfers between devices, local(): lax.all_to_all(served, 'shard', split_axis=0, concat_axis=0, tiled=True)  10.7 us
    pallas_call x1, Pallas kernels, serve(): pl.pallas_call(serve_kernel, grid=(peers // step,), in_specs=[pl.BlockSpe...  9.8 us
  transfers between devices with their start and end apart: 4, of which 4 were waited for; matrix products, arithmetic and copies ran while one was open for 2% of the time, Pallas kernels for 0%

profile of v2, /device:TPU:2, one launch (start us, length us, event | category | flops | bytes accessed | tf_op | source)
XLA Modules:
  0.0 268.6 jit_solution(13570204918266469128)
XLA Ops:
  7.2 0.0 copy-start.3
  7.2 0.0 all-gather.2.cloned.1.call-start
  7.2 1.1 copy.26
  8.4 0.1 fusion.9
  8.5 0.1 fusion.8
  8.6 0.9 concatenate.10
  9.5 0.0 all-gather.2.cloned.1.call-update
  9.5 0.0 copy-done.3
  9.5 0.1 copy.27
  9.6 20.5 %all_to_all.21 = s32[64,1,48]{2,1,0:T(1,128)} all-to-all(s32[64,1,48]{2,1,0:T(1,128)S(1)} %bitcast.7), channel_id=1, replica_groups=mesh['shard'=64,'rep'=4] {'shard'}, dimensions={0} | all-to-all | bytes 24576 | tf_op jit(solution)/shard_map/all_to_all | solution.py:293
  30.2 11.6 %all-gather.2.cloned.1.call-done.slab_ref = bf16[1536,512]{1,0:T(8,128)(2,1)} async-done(((bf16[384,512]{1,0:T(8,128)(2,1)}), bf16[1536,512]{1,0:T(8,128)(2,1)}) %all-gather.2.cloned.1.call-update) | async-done | bytes 1572880 | tf_op jit(solution)/shard_map/all_gather | solution.py:294
  41.8 9.8 %serve.1 = bf16[64,160,128]{2,1,0:T(8,128)(2,1)} custom-call(s32[64,48]{1,0:T(8,128)} %bitcast.6, bf16[1536,512]{1,0:T(8,128)(2,1)} %all-gather.2.cloned.1.call-done.slab_ref), custom_call_target="tpu_custom_call" | custom-call | tf_op jit(solution)/shard_map/serve/pallas_call | solution.py:65
  51.6 0.0 copy-start.6
  51.6 0.0 copy-start.5
  51.6 10.7 %all-to-all-start.1 = ((bf16[64,160,128]{2,1,0:T(8,128)(2,1)}), bf16[64,160,128]{2,1,0:T(8,128)(2,1)S(1)}, u32[]{:S(2)}, u32[]{:S(2)}) async-start(bf16[64,160,128]{2,1,0:T(8,128)(2,1)} %serve.1), calls=%async_computation.1 | async-start | bytes 5242880 | tf_op jit(solution)/shard_map/all_to_all | solution.py:296
  62.3 1.2 copy.28
  63.5 0.0 copy-done.6
  63.5 0.6 gather_fusion
  64.1 0.1 slice.44
  64.2 0.0 copy-done.5
  64.2 0.6 select_maximum_fusion.rel_ref
  64.8 58.1 %all-to-all-done.1.fetched_ref = bf16[64,160,128]{2,1,0:T(8,128)(2,1)S(1)} async-done(((bf16[64,160,128]{2,1,0:T(8,128)(2,1)}), bf16[64,160,128]{2,1,0:T(8,128)(2,1)S(1)}, u32[]{:S(2)}, u32[]{:S(2)}) %all-to-all-start.1) | async-done | bytes 2621472 | tf_op jit(solution)/shard_map/all_to_all | solution.py:296
  122.9 0.0 copy-start
  122.9 1.5 copy-done
  124.4 29.0 %edges.1 = bf16[64,160,128]{2,1,0:T(8,128)(2,1)} custom-call(s32[3,512]{1,0:T(4,128)} %head_ids.1, s32[3,512]{1,0:T(4,128)} %tail_ids.1, s32[3,512]{1,0:T(4,128)} %neg_ids.1, f32[3,512]{1,0:T(4,128)} %select_maximum_fusion.rel_ref, bf16[64,160,128]{2,1,0:T(8,128)(2,1)} %copy-done), custom_call_target="tpu_custom_call" | custom-call | tf_op jit(solution)/shard_map/edges/pallas_call | solution.py:272
  153.4 0.0 copy-start.2
  153.4 7.5 %all-to-all-start.2 = ((bf16[64,160,128]{2,1,0:T(8,128)(2,1)}), bf16[64,160,128]{2,1,0:T(8,128)(2,1)S(1)}, u32[]{:S(2)}, u32[]{:S(2)}) async-start(bf16[64,160,128]{2,1,0:T(8,128)(2,1)} %edges.1), calls=%async_computation.2 | async-start | bytes 5242880 | tf_op jit(solution)/shard_map/all_to_all | solution.py:299
  160.9 0.0 reduce-scatter.2.cloned.1.call-start
  161.0 0.5 broadcast.49
  161.5 0.0 copy-done.2
  161.5 0.7 reduce.3
  162.2 0.7 reshape.39.wanted_ref
  162.9 0.0 copy-start.4
  162.9 58.6 %all-to-all-done.2.rows_ref = bf16[64,160,128]{2,1,0:T(8,128)(2,1)S(1)} async-done(((bf16[64,160,128]{2,1,0:T(8,128)(2,1)}), bf16[64,160,128]{2,1,0:T(8,128)(2,1)S(1)}, u32[]{:S(2)}, u32[]{:S(2)}) %all-to-all-start.2) | async-done | bytes 2621472 | tf_op jit(solution)/shard_map/all_to_all | solution.py:299
  221.5 0.0 copy-start.1
  221.5 1.5 copy-done.1
  223.0 9.4 %collect.1 = bf16[1536,512]{1,0:T(8,128)(2,1)} custom-call(s32[24,128]{1,0:T(8,128)} %reshape.39.wanted_ref, bf16[64,160,128]{2,1,0:T(8,128)(2,1)} %copy-done.1), custom_call_target="tpu_custom_call" | custom-call | tf_op jit(solution)/shard_map/collect/pallas_call | solution.py:115
  232.4 0.0 reduce-scatter.2.cloned.1.call-update
  232.4 25.2 %reduce-scatter.2.cloned.1.call-done = bf16[384,512]{1,0:T(8,128)(2,1)} async-done(((bf16[1536,512]{1,0:T(8,128)(2,1)}), bf16[384,512]{1,0:T(8,128)(2,1)}) %reduce-scatter.2.cloned.1.call-update) | async-done | bytes 393232 | tf_op jit(solution)/shard_map/reduce_scatter | solution.py:301
  257.6 1.1 fusion.7
  258.7 1.0 fusion.6
  259.7 0.3 fusion.3
  260.0 0.0 copy-done.4
  260.0 0.6 fusion.5
  260.6 0.3 fusion.2
  260.9 0.9 copy.33
  (5 shorter events, 0.0 us)
Async XLA Ops:
  7.2 2.4 copy-start.3
  7.2 34.6 %all-gather.2.cloned.1.call-start = ((), (), s32[]{:S(2)}) async-start(), calls=%async_computation.4 | async-start | bytes 1966080 | tf_op jit(solution)/shard_map/all_gather | solution.py:294
  51.6 11.9 %copy-start.6 = (s32[1,3]{1,0:T(1,128)S(1)}, s32[1,3]{1,0:T(1,128)}, u32[]{:S(2)}) copy-start(s32[1,3]{1,0:T(1,128)} %param.15) | copy-start | bytes 40
  51.6 12.6 %copy-start.5 = (pred[256]{0:T(512)(128)(4,1)S(1)}, pred[256]{0:T(512)(128)(4,1)}, u32[]{:S(2)}) copy-start(pred[256]{0:T(512)(128)(4,1)} %constant.3.clone.1) | copy-start | bytes 772
  51.6 71.3 %all-to-all-start.1 = ((bf16[64,160,128]{2,1,0:T(8,128)(2,1)}), bf16[64,160,128]{2,1,0:T(8,128)(2,1)S(1)}, u32[]{:S(2)}, u32[]{:S(2)}) async-start(bf16[64,160,128]{2,1,0:T(8,128)(2,1)} %serve.1), calls=%async_computation.1 | async-start | bytes 5242880 | tf_op jit(solution)/shard_map/all_to_all | solution.py:296
  122.9 1.5 copy-start
  153.4 8.1 %copy-start.2 = (s32[64,1,48]{2,1,0:T(1,128)S(1)}, s32[64,1,48]{2,1,0:T(1,128)}, u32[]{:S(2)}) copy-start(s32[64,1,48]{2,1,0:T(1,128)} %all_to_all.21) | copy-start | bytes 36868
  153.4 68.1 %all-to-all-start.2 = ((bf16[64,160,128]{2,1,0:T(8,128)(2,1)}), bf16[64,160,128]{2,1,0:T(8,128)(2,1)S(1)}, u32[]{:S(2)}, u32[]{:S(2)}) async-start(bf16[64,160,128]{2,1,0:T(8,128)(2,1)} %edges.1), calls=%async_computation.2 | async-start | bytes 5242880 | tf_op jit(solution)/shard_map/all_to_all | solution.py:299
  160.9 96.7 %reduce-scatter.2.cloned.1.call-start = ((), (), s32[]{:S(2)}) async-start(), calls=%async_computation.5 | async-start | bytes 1966080 | tf_op jit(solution)/shard_map/reduce_scatter | solution.py:301
  162.9 97.1 %copy-start.4 = (f32[384]{0:T(512)S(1)}, f32[384]{0:T(512)}, u32[]{:S(2)}) copy-start(f32[384]{0:T(512)} %param.9) | copy-start | bytes 4612
  221.5 1.5 copy-start.1
Sparse Core Ops, SparseCore 0:
  9.8 31.9 all-gather.1
  232.5 25.0 reduce-scatter.1
